TPU v7x, 32 devices: a whole 2x2x4 slice. The times are simulated.
32 devices in a mesh: row: 4 (over y, core), col: 4 (over z), rep: 2 (over x).
Axes of the slice: x: 2, y: 2, z: 4, core: 2. Of those that a mesh axis runs over, the one named last changes fastest.
Arguments:
- precision: float32 [12288, 12288], P('row', 'col'), may hold values from -1 to 4, as said below
- samples: float32 [1024, 12288], P('rep', 'col'), may hold values from -6 to 6
- new_rows: float32 [512, 12288], P(None, 'row'), may hold values from -6 to 6
- ngram_order: int32 [12288], replicated, may hold values from 1 to 3
Outputs:
- updated: float32 [12288, 12288], P('row', ('col', 'rep'))
- residuals: float32 [512, 12288], P('row', ('col', 'rep'))
Inputs may be any that keep to these rules, and one draw needn't show every extreme that they name: `precision`: symmetric; diagonal entries from 1 to 4, off-diagonal entries of magnitude at most 9 / sqrt(12288).
All inputs are finite; a program needn't handle non-finite values.
Results may differ from a plain program's by a relative error of at most 0.0003.
Values sent between devices are 32-bit elements; how exact they have to be, the bound alone decides.
A program may use at most 192 MiB of HBM per device.

v0:
```python
import functools

import jax
import jax.numpy as jnp
from jax import lax
from jax.experimental import pallas as pl
from jax.experimental.pallas import tpu as pltpu
from jax.sharding import PartitionSpec as P

step_size = 0.25
penalty = 0.08
MESH = pl.DeviceIdType.MESH
F32 = jnp.float32
BF16 = jnp.bfloat16
step_rows = 128
chunk_rows = 64
depth = 256


def block_of(size):
    for block in (512, 384, 256, 128):
        if size % block == 0:
            return block
    return size


def split(values):
    high = values.astype(BF16)
    return high, (values - high.astype(F32)).astype(BF16)


def dot(left, right):
    return jnp.dot(left, right, preferred_element_type=F32)


def aligned(start, size, unit):
    return pl.ds(pl.multiple_of(start, unit), size)


def gather_kernel(
    R, C, S, TR, TC, H,
    prec, samp,
    acc_out, x_near, x_far, y_near, y_far, y_cols, x_cols_far, y_cols_far,
    acc, left, right, right_high, right_low, x_rows, partial, arrived, reduced,
    up_send, down_send, side_send, near_recv, far_recv,
    rs_send, rs_recv, ag_send, ag_recv, own_copy,
    xq_send, xq_recv, xf_send, xf_recv, yq_send, yq_recv, yf_send, yf_recv,
    om_sem, load_sem, out_sem,
):
    r, z, p = lax.axis_index("row"), lax.axis_index("col"), lax.axis_index("rep")
    ratio = TC // TR
    other = 1 - p
    source = r // ratio
    offset = (r % ratio) * TR
    is_source = z == source
    has_up = jnp.logical_and(z >= source, z < C - 1)
    has_down = jnp.logical_and(z <= source, z > 0)
    steps = S // step_rows
    chunks = S // chunk_rows
    per_step = step_rows // chunk_rows
    piece = step_rows // R
    quarter = S // R
    own_cols = aligned(p * H, H, 128)
    far_cols = aligned(other * H, H, 128)
    tile_cols = aligned(offset, TR, 128)

    def mate(d):
        return lax.rem(r + d, R)

    def remote(src, dst, send, recv, where):
        return pltpu.make_async_remote_copy(
            src_ref=src, dst_ref=dst, send_sem=send, recv_sem=recv, device_id=where, device_id_type=MESH
        )

    across = (r, z, other)

    barrier = pltpu.get_barrier_semaphore()
    pl.semaphore_signal(barrier, inc=1, device_id=across, device_id_type=MESH)
    for d in range(1, R):
        pl.semaphore_signal(barrier, inc=1, device_id=(mate(d), z, p), device_id_type=MESH)

    for hop in (1, C - 1):
        pl.semaphore_signal(barrier, inc=1, device_id=(r, lax.rem(z + hop, C), p), device_id_type=MESH)
    pl.semaphore_wait(barrier, R + 2)

    kinds = ((samp, x_near, x_far), (y_cols, y_near, y_far))

    def near_copies(kind, i, wide):
        wide_ref, near, far = kinds[kind]
        rows = aligned(i * chunk_rows, chunk_rows, chunk_rows)
        src = wide_ref.at[rows, tile_cols] if wide else near.at[rows]
        up = remote(src, near.at[rows], up_send.at[kind, i], near_recv.at[kind, i], (r, z + 1, p))
        down = remote(src, near.at[rows], down_send.at[kind, i], near_recv.at[kind, i], (r, z - 1, p))
        side = remote(src, far.at[rows], side_send.at[kind, i], far_recv.at[kind, i], across)
        return up, down, side

    def pass_on(kind, i, wide):
        up, down, side = near_copies(kind, i, wide)

        @pl.when(has_up)
        def _():
            up.start()

        @pl.when(has_down)
        def _():
            down.start()

        side.start()

    def start_source(kind, i):
        @pl.when(is_source)
        def _():
            pass_on(kind, i, True)

    def serve(kind, i):
        @pl.when(jnp.logical_not(is_source))
        def _():
            near_copies(kind, i, False)[0].wait_recv()
            pass_on(kind, i, False)

    def wait_far(kind, i):
        near_copies(kind, i, False)[2].wait_recv()

    def wait_sent(kind, i):
        up, down, side = near_copies(kind, i, False)

        @pl.when(has_up)
        def _():
            up.wait_send()

        @pl.when(has_down)
        def _():
            down.wait_send()

        side.wait_send()

    def xq_copy():
        rows = aligned(r * quarter, quarter, 8)
        return remote(samp.at[rows, far_cols], x_cols_far.at[rows], xq_send, xq_recv, across)

    def xf_copy(d, sender):
        rows = aligned(sender * quarter, quarter, 8)
        return remote(x_cols_far.at[rows], x_cols_far.at[rows], xf_send.at[d], xf_recv.at[d], (mate(d), z, p))

    def rs_copy(s, slot, d):
        rows = aligned(mate(d) * piece, piece, 8)
        return remote(
            partial.at[slot, rows], arrived.at[s, d - 1], rs_send.at[s, d], rs_recv.at[s, d], (mate(d), z, p)
        )

    def step_piece(s, sender):
        return aligned(s * step_rows + sender * piece, piece, 8)

    def ag_copy(s, d, sender):
        return remote(
            reduced.at[s], y_cols.at[step_piece(s, sender)], ag_send.at[s, d], ag_recv.at[s, d], (mate(d), z, p)
        )

    def own_piece(s):
        return pltpu.make_async_copy(reduced.at[s], y_cols.at[step_piece(s, r)], own_copy.at[s])

    def yq_copy(s):
        return remote(
            reduced.at[s, :, far_cols], y_cols_far.at[step_piece(s, r)], yq_send.at[s], yq_recv.at[s], across
        )

    def yf_copy(s, d, sender):
        rows = step_piece(s, sender)
        return remote(y_cols_far.at[rows], y_cols_far.at[rows], yf_send.at[s, d], yf_recv.at[s, d], (mate(d), z, p))

    for i in range(chunks):
        start_source(0, i)
    xq_copy().start()

    def om_copy(b, slot):
        rows = aligned(b * depth, depth, depth)
        return pltpu.make_async_copy(prec.at[rows], left.at[slot, :, pl.ds(0, TC)], om_sem.at[slot])

    blocks = TR // depth
    wide_block = block_of(TC)

    def finish_rs(s, slot):
        for d in range(1, R):
            rs_copy(s, slot, d).wait_recv()
        total = partial[slot, aligned(r * piece, piece, 8)]
        for d in range(1, R):
            total = total + arrived[s, d - 1]
        reduced[s] = total
        own_piece(s).start()
        yq_copy(s).start()
        for d in range(1, R):
            ag_copy(s, d, r).start()

    def wait_ag(s):
        own_piece(s).wait()
        for d in range(1, R):
            ag_copy(s, d, lax.rem(r + R - d, R)).wait_recv()

    def source_step(s):
        for j in range(per_step):
            start_source(1, s * per_step + j)

    def forward_yf(s):
        yq_copy(s).wait_recv()
        for d in range(1, R):
            yf_copy(s, d, r).start()

    @pl.loop(0, steps)
    def _(s):
        slot = lax.rem(s, 2)
        om_copy(0, 0).start()
        for j in range(per_step):
            serve(0, s * per_step + j)
        rows = aligned(s * step_rows, step_rows, step_rows)

        @pl.when(is_source)
        def _():
            pltpu.make_async_copy(samp.at[rows, tile_cols], x_rows, load_sem.at[0]).start()

        @pl.when(jnp.logical_not(is_source))
        def _():
            pltpu.make_async_copy(x_near.at[rows], x_rows, load_sem.at[0]).start()

        @pl.when(s >= 2)
        def _():
            for d in range(1, R):
                rs_copy(s - 2, slot, d).wait_send()

        pltpu.make_async_copy(x_near.at[rows], x_rows, load_sem.at[0]).wait()

        @pl.loop(0, blocks)
        def _(b):
            here = lax.rem(b, 2)
            om_copy(b, here).wait()

            @pl.when(b + 1 < blocks)
            def _():
                om_copy(b + 1, 1 - here).start()

            high, low = split(x_rows[:, aligned(b * depth, depth, depth)])
            both = jnp.concatenate([high, low], axis=0)
            for n in range(TC // wide_block):
                cols = pl.ds(n * wide_block, wide_block)
                w_high, w_low = split(left[here, :, cols])
                pair = dot(both, w_high)
                value = pair[:step_rows] + pair[step_rows:] + dot(high, w_low)

                @pl.when(b == 0)
                def _():
                    partial[slot, :, cols] = value

                @pl.when(b > 0)
                def _():
                    partial[slot, :, cols] += value

        for d in range(1, R):
            rs_copy(s, slot, d).start()

        @pl.when(s >= 1)
        def _():
            finish_rs(s - 1, 1 - slot)

        @pl.when(s == 1)
        def _():
            xq_copy().wait_recv()
            for d in range(1, R):
                xf_copy(d, r).start()

        @pl.when(s >= 2)
        def _():
            wait_ag(s - 2)
            source_step(s - 2)
            forward_yf(s - 2)

    last = steps - 1
    serve(1, 0)
    serve(1, 1)
    finish_rs(last, last % 2)
    wait_ag(last - 1)
    source_step(last - 1)
    forward_yf(last - 1)
    serve(1, 2)
    wait_ag(last)
    source_step(last)
    serve(1, 3)
    forward_yf(last)

    m_block, n_block = block_of(TR), block_of(H)
    out_blocks = TR // m_block
    halves = S // depth
    group = depth // chunk_rows

    def out_copy(i):
        rows = aligned(i * m_block, m_block, m_block)
        return pltpu.make_async_copy(acc.at[rows], acc_out.at[rows], out_sem)

    def load(src_left, src_right):
        pltpu.make_async_copy(src_left, left.at[0, :, pl.ds(0, TR)], load_sem.at[0]).start()
        pltpu.make_async_copy(src_right, right, load_sem.at[1]).start()

    def near_ref(kind, rows):
        def run(src_right):
            @pl.when(is_source)
            def _():
                load(kinds[kind][0].at[rows, tile_cols], src_right)

            @pl.when(jnp.logical_not(is_source))
            def _():
                load(kinds[kind][1].at[rows], src_right)

        return run

    def begin(u):
        if u == 2:
            for s in range(steps):
                for d in range(1, R):
                    yf_copy(s, d, lax.rem(r + R - d, R)).wait_recv()
        if u == 5:
            for d in range(1, R):
                xf_copy(d, lax.rem(r + R - d, R)).wait_recv()
        served = {1: (4,), 3: (5,), 5: (6, 7)}.get(u, ())
        for i in served:
            serve(1, i)
        if u in (2, 3):
            for i in range(group):
                wait_far(0, (u - 2) * group + i)
        if u in (5, 7):
            for i in range(group):
                wait_far(1, (u - 5) // 2 * group + i)
        k = u % 2 if u < 4 else (u - 4) // 2
        rows = pl.ds(k * depth, depth)
        if u < 2:
            near_ref(0, rows)(y_cols.at[rows, own_cols])
        elif u < 4:
            load(x_far.at[rows], y_cols_far.at[rows])
        elif u % 2 == 0:
            near_ref(1, rows)(samp.at[rows, own_cols])
        else:
            load(y_far.at[rows], x_cols_far.at[rows])

    assert halves == 2 and chunks == 8 and per_step == 2

    @pl.loop(0, 8)
    def _(u):
        for case in range(8):
            @pl.when(u == case)
            def _(case=case):
                begin(case)

        pltpu.make_async_copy(x_far.at[pl.ds(0, depth)], left.at[0, :, pl.ds(0, TR)], load_sem.at[0]).wait()
        pltpu.make_async_copy(y_cols_far.at[pl.ds(0, depth)], right, load_sem.at[1]).wait()
        high, low = split(right[...])
        right_high[...] = high
        right_low[...] = low

        @pl.loop(0, out_blocks)
        def _(i):
            rows = aligned(i * m_block, m_block, m_block)
            l_high, l_low = split(left[0, :, rows].T)
            for n in range(H // n_block):
                cols = pl.ds(n * n_block, n_block)
                value = dot(l_high, right_high[:, cols]) + dot(l_low, right_high[:, cols])
                value = value + dot(l_high, right_low[:, cols])

                @pl.when(u == 0)
                def _():
                    acc[rows, cols] = value

                @pl.when(u > 0)
                def _():
                    acc[rows, cols] += value

            @pl.when(u == 7)
            def _():
                out_copy(i).start()

    @pl.loop(0, chunks)
    def _(i):
        wait_sent(0, i)
        wait_sent(1, i)

    xq_copy().wait_send()
    for d in range(1, R):
        xf_copy(d, r).wait_send()
    for s in range(steps):
        yq_copy(s).wait_send()
        for d in range(1, R):
            if s >= steps - 2:
                rs_copy(s, s % 2, d).wait_send()
            ag_copy(s, d, r).wait_send()
            yf_copy(s, d, r).wait_send()

    @pl.loop(0, out_blocks)
    def _(i):
        out_copy(i).wait()


def gathered(precision, samples, R, C):
    TR, TC = precision.shape
    S = samples.shape[0]
    H = TC // 2
    assert C > 2
    steps, chunks = S // step_rows, S // chunk_rows
    piece = step_rows // R
    wide = max(TR, TC)
    dma = pltpu.SemaphoreType.DMA
    shapes = [(TR, H), (S, TR), (S, TR), (S, TR), (S, TR), (S, TC), (S, H), (S, H)]
    return pl.pallas_call(
        functools.partial(gather_kernel, R, C, S, TR, TC, H),
        out_shape=[jax.ShapeDtypeStruct(shape, F32) for shape in shapes],
        in_specs=[pl.BlockSpec(memory_space=pl.ANY)] * 2,
        out_specs=[pl.BlockSpec(memory_space=pl.ANY)] * len(shapes),
        scratch_shapes=[
            pltpu.VMEM((TR, H), F32),
            pltpu.VMEM((2, depth, wide), F32),
            pltpu.VMEM((depth, H), F32),
            pltpu.VMEM((depth, H), BF16),
            pltpu.VMEM((depth, H), BF16),
            pltpu.VMEM((step_rows, TR), F32),
            pltpu.VMEM((2, step_rows, TC), F32),
            pltpu.VMEM((steps, R - 1, piece, TC), F32),
            pltpu.VMEM((steps, piece, TC), F32),
            dma((2, chunks)), dma((2, chunks)), dma((2, chunks)), dma((2, chunks)), dma((2, chunks)),
            dma((steps, R)), dma((steps, R)), dma((steps, R)), dma((steps, R)), dma((steps,)),
            dma, dma, dma((R,)), dma((R,)), dma((steps,)), dma((steps,)), dma((steps, R)), dma((steps, R)),
            dma((2,)), dma((2,)), dma,
        ],
        compiler_params=pltpu.CompilerParams(
            collective_id=0, has_side_effects=True, vmem_limit_bytes=60 * 2**20
        ),
        name="gather_symmetric",
    )(precision, samples)[0]


def update_kernel(samples_total, block, ids, sym, prec, rows_o, cols_o, new_t, out, res):
    i = pl.program_id(0)
    M, H = sym.shape
    row_id = ids[0] + i * block + lax.broadcasted_iota(jnp.int32, (M, H), 0)
    col_id = ids[1] + lax.broadcasted_iota(jnp.int32, (M, H), 1)
    on_diagonal = row_id == col_id
    held = prec[...]
    inverse = jnp.where(on_diagonal, 1.0 / jnp.where(on_diagonal, held, 1.0), 0.0)
    gradient = sym[...] / (2.0 * samples_total) - inverse
    stepped = held - step_size * gradient
    threshold = step_size * penalty * 0.5 * (rows_o[...] + cols_o[...])
    size = jnp.maximum(jnp.abs(stepped) - threshold, 0.0)
    shrunk = jnp.where(stepped < 0.0, -size, size)
    updated = jnp.where(on_diagonal, stepped, shrunk)
    out[...] = updated
    u_high, u_low = split(updated)
    n_high, n_low = split(new_t[...])
    count = n_high.shape[0]
    pair = dot(jnp.concatenate([n_high, n_low], axis=0), u_high)
    value = pair[:count] + pair[count:] + dot(n_high, u_low)
    diag = jnp.sum(jnp.where(on_diagonal, held, 0.0), axis=0, keepdims=True)
    diag = jnp.broadcast_to(diag, (8, H))

    @pl.when(i == 0)
    def _():
        res[pl.ds(0, count), :] = value
        res[pl.ds(count, 8), :] = diag

    @pl.when(i > 0)
    def _():
        res[pl.ds(0, count), :] += value
        res[pl.ds(count, 8), :] += diag


def updated_and_partial(symmetric, precision, new_rows, orders_rows, orders_cols, ids, half_index, samples_total):
    TR, H = symmetric.shape
    count = new_rows.shape[0]
    block = 256
    return pl.pallas_call(
        functools.partial(update_kernel, samples_total, block),
        out_shape=[jax.ShapeDtypeStruct((TR, H), F32), jax.ShapeDtypeStruct((count + 8, H), F32)],
        grid_spec=pltpu.PrefetchScalarGridSpec(
            num_scalar_prefetch=1,
            grid=(TR // block,),
            in_specs=[
                pl.BlockSpec((block, H), lambda i, ids: (i, 0)),
                pl.BlockSpec((block, H), lambda i, ids: (i, ids[2])),
                pl.BlockSpec((block, 1), lambda i, ids: (i, 0)),
                pl.BlockSpec((1, H), lambda i, ids: (0, 0)),
                pl.BlockSpec((count, block), lambda i, ids: (0, i)),
            ],
            out_specs=[
                pl.BlockSpec((block, H), lambda i, ids: (i, 0)),
                pl.BlockSpec((count + 8, H), lambda i, ids: (0, 0)),
            ],
        ),
        compiler_params=pltpu.CompilerParams(vmem_limit_bytes=56 * 2**20),
        name="update_rows",
    )(ids, symmetric, precision, orders_rows, orders_cols, new_rows)


def residual_kernel(R, part, out, held, got, diags, send, recv, diag_send, diag_recv):
    r, z, p = lax.axis_index("row"), lax.axis_index("col"), lax.axis_index("rep")
    rows = out.shape[0]
    rounds = R.bit_length() - 1

    def flip(bit):
        low = lax.rem(r // bit, 2)
        return r + bit - 2 * bit * low

    barrier = pltpu.get_barrier_semaphore()
    for d in range(1, R):
        where = (lax.rem(r + d, R), z, p)
        pl.semaphore_signal(barrier, inc=1, device_id=where, device_id_type=MESH)
    pl.semaphore_wait(barrier, R - 1)

    def diag_copy(d):
        where = (lax.rem(r + d, R), z, p)
        return pltpu.make_async_remote_copy(
            src_ref=part.at[pl.ds(rows * R, 8)], dst_ref=diags.at[d - 1], send_sem=diag_send.at[d],
            recv_sem=diag_recv.at[d], device_id=where, device_id_type=MESH)

    def exchange(stage, j):
        bit = 1 << stage
        peer = flip(bit)
        block = lax.rem(peer, 2 * bit) + 2 * bit * j
        src = part if stage == 0 else held
        return pltpu.make_async_remote_copy(
            src_ref=src.at[aligned(block * rows, rows, 8)], dst_ref=got.at[stage, j],
            send_sem=send.at[stage, j], recv_sem=recv.at[stage, j],
            device_id=(peer, z, p), device_id_type=MESH)

    count = [R >> (stage + 1) for stage in range(rounds)]
    for stage in range(rounds):
        bit = 1 << stage
        if stage == 0:
            for j in range(count[0]):
                exchange(0, j).start()
            for d in range(1, R):
                diag_copy(d).start()

        def receive(j, stage=stage, bit=bit):
            mine = lax.rem(r, 2 * bit) + 2 * bit * j
            block = aligned(mine * rows, rows, 8)
            exchange(stage, j).wait_recv()
            src = part if stage == 0 else held
            held[block] = src[block] + got[stage, j]

        for j in range(count[stage]):
            receive(j)
        if stage + 1 < rounds:
            for j in range(count[stage + 1]):
                exchange(stage + 1, j).start()
    diag = part[pl.ds(rows * R, 1)]
    for d in range(1, R):
        diag_copy(d).wait_recv()
        diag = diag + diags[d - 1, pl.ds(0, 1)]
    out[...] = held[aligned(r * rows, rows, 8)] / diag
    for stage in range(rounds):
        for j in range(count[stage]):
            exchange(stage, j).wait_send()
    for d in range(1, R):
        diag_copy(d).wait_send()


def residual_sum(part, R):
    total, H = part.shape
    rows = (total - 8) // R
    assert R & (R - 1) == 0
    rounds = R.bit_length() - 1
    dma = pltpu.SemaphoreType.DMA
    return pl.pallas_call(
        functools.partial(residual_kernel, R),
        out_shape=jax.ShapeDtypeStruct((rows, H), F32),
        in_specs=[pl.BlockSpec(memory_space=pltpu.VMEM)],
        out_specs=pl.BlockSpec(memory_space=pltpu.VMEM),
        scratch_shapes=[
            pltpu.VMEM((R * rows, H), F32),
            pltpu.VMEM((rounds, R // 2, rows, H), F32),
            pltpu.VMEM((R - 1, 8, H), F32),
            dma((rounds, R // 2)), dma((rounds, R // 2)), dma((R,)), dma((R,)),
        ],
        compiler_params=pltpu.CompilerParams(
            collective_id=1, has_side_effects=True, vmem_limit_bytes=40 * 2**20
        ),
        name="residual_sum",
    )(part)


def per_device(precision, samples, new_rows, ngram_order):
    R, C, reps = lax.axis_size("row"), lax.axis_size("col"), lax.axis_size("rep")
    r, c, p = lax.axis_index("row"), lax.axis_index("col"), lax.axis_index("rep")
    TR, TC = precision.shape
    H = TC // reps
    assert reps == 2 and TC % TR == 0 and R * TR == C * TC
    symmetric = gathered(precision, samples, R, C)
    orders = ngram_order.astype(F32)
    row_start, col_start = r * TR, c * TC + p * H
    order_rows = lax.dynamic_slice_in_dim(orders, row_start, TR, 0)[:, None]
    order_cols = lax.dynamic_slice_in_dim(orders, col_start, H, 0)[None, :]
    ids = jnp.stack([row_start, col_start, p]).astype(jnp.int32)
    updated, part = updated_and_partial(
        symmetric, precision, new_rows, order_rows, order_cols, ids, p, samples.shape[0] * reps
    )
    return updated, residual_sum(part, R)


def solution(mesh):
    placed = (P("row", "col"), P("rep", "col"), P(None, "row"), P())
    return jax.shard_map(
        per_device,
        mesh=mesh,
        in_specs=placed,
        out_specs=(P("row", ("col", "rep")), P("row", ("col", "rep"))),
        check_vma=False,
    )
```

profile of v0, /device:TPU:0, one launch (start us, length us, event | category | flops | bytes accessed | tf_op | source)
XLA Modules:
  0.0 490.3 jit_solution(7324723368109939857)
XLA Ops:
  0.6 0.6 pad_add_fusion.ids
  1.2 0.0 copy-start.1
  1.3 401.9 %gather_symmetric.1 = (f32[3072,1536]{1,0:T(8,128)}, f32[512,3072]{1,0:T(8,128)}, f32[512,3072]{1,0:T(8,128)}, f32[512,3072]{1,0:T(8,128)}, f32[512,3072]{1,0:T(...) custom-call(f32[3072,3072]{1,0:T(8,128)} %prec.3, f32[512,3072]{1,0:T(8,128)} %samp.1), custom_call_target="tpu_custom_call" | custom-call | tf_op jit(solution)/shard_map/gather_symmetric/pallas_call | solution.py:408
  403.2 0.0 copy-done.1
  403.2 1.7 copy.6.rows_o
  405.0 0.1 dynamic_slice.7
  405.0 0.6 broadcast_in_dim.7.cols_o
  405.6 35.0 %update_rows.1 = (f32[3072,1536]{1,0:T(8,128)}, f32[520,1536]{1,0:T(8,128)}) custom-call(s32[3]{0:T(128)} %pad_add_fusion.ids, f32[3072,1536]{1,0:T(8,128)} %get-tuple-element.5.sym, f32[3072,3072]{1,0:T(8,128)} %prec.3, f32[3072,1]{1,0:T(8,128)} %copy.6.rows_o, f32[1,1536]{1,0:T(1,128)} %broadcast_in_dim.7.cols_o, f32[512,3072]{1,0:T(8,128)} %new_t.1), custom_call_target="tpu_custom_call" | custom-call | tf_op jit(solution)/shard_map/update_rows/pallas_call | solution.py:473
  440.7 0.0 copy-start
  440.7 1.9 copy-done
  442.6 46.8 %residual_sum.1 = f32[128,1536]{1,0:T(8,128)S(1)} custom-call(f32[520,1536]{1,0:T(8,128)S(1)} %copy-done), custom_call_target="tpu_custom_call" | custom-call | tf_op jit(solution)/shard_map/residual_sum/pallas_call | solution.py:566
  489.4 0.9 copy.8
  (2 shorter events, 0.0 us)
Async XLA Ops:
  1.2 402.0 %copy-start.1 = (s32[12288]{0:T(1024)S(1)}, s32[12288]{0:T(1024)}, u32[]{:S(2)}) copy-start(s32[12288]{0:T(1024)} %param.7) | copy-start | bytes 147460
  440.7 1.9 copy-start
where the time goes:
time: 493 us; the launch traced here: 490 us
  Pallas kernels  484 us (98%)
  local copies, waits for them, and re-layouts  5.19 us (1%)
    pallas_call x1, Pallas kernels, gathered(): pl.pallas_call(functools.partial(gather_kernel, R, C, S, TR, TC, H), out_...  402 us
    pallas_call x1, Pallas kernels, residual_sum(): pl.pallas_call(functools.partial(residual_kernel, R), out_shape=jax.Shape...  46.8 us
    pallas_call x1, Pallas kernels, updated_and_partial(): pl.pallas_call(functools.partial(update_kernel, samples_total, block), ou...  35 us

commit v1 on v0

--- a/solution.py
+++ b/solution.py
@@ -12,14 +12,15 @@
 MESH = pl.DeviceIdType.MESH
 F32 = jnp.float32
 BF16 = jnp.bfloat16
-step_rows = 128
+step_rows = 256
 chunk_rows = 64
 depth = 256
-
-
-def block_of(size):
-    for block in (512, 384, 256, 128):
-        if size % block == 0:
+alternate = ((0, 5), (0, 7))
+
+
+def block_of(size, most=512):
+    for block in (1024, 768, 512, 384, 256, 128):
+        if block <= most and size % block == 0:
             return block
     return size
 
@@ -40,11 +41,12 @@
 def gather_kernel(
     R, C, S, TR, TC, H,
     prec, samp,
-    acc_out, x_near, x_far, y_near, y_far, y_cols, x_cols_far, y_cols_far,
-    acc, left, right, right_high, right_low, x_rows, partial, arrived, reduced,
-    up_send, down_send, side_send, near_recv, far_recv,
-    rs_send, rs_recv, ag_send, ag_recv, own_copy,
-    xq_send, xq_recv, xf_send, xf_recv, yq_send, yq_recv, yf_send, yf_recv,
+    acc_out, x_near, x_far, y_near, y_far, y_cols, x_cols_far, y_cols_far, kept_rows,
+    acc, left, right, right_high, right_low, x_rows, partial, paired, mid, arrived, reduced,
+    up_send, down_send, side_send, near_recv, far_recv, alt_up, alt_down, alt_over, alt_recv,
+    pair_send, pair_recv, rs_send, rs_recv, own_copy,
+    share_send, share_recv, hand_send, hand_recv,
+    xq_send, xq_recv, yq_send, yq_recv,
     om_sem, load_sem, out_sem,
 ):
     r, z, p = lax.axis_index("row"), lax.axis_index("col"), lax.axis_index("rep")
@@ -55,6 +57,12 @@
     is_source = z == source
     has_up = jnp.logical_and(z >= source, z < C - 1)
     has_down = jnp.logical_and(z <= source, z > 0)
+    alt = lax.rem(r + R // 2, R)
+    alt_source = alt // ratio
+    is_alt_source = z == alt_source
+    alt_has_up = jnp.logical_and(z >= alt_source, z < C - 1)
+    alt_has_down = jnp.logical_and(z <= alt_source, z > 0)
+    alt_cols = aligned((alt % ratio) * TR, TR, 128)
     steps = S // step_rows
     chunks = S // chunk_rows
     per_step = step_rows // chunk_rows
@@ -64,8 +72,19 @@
     far_cols = aligned(other * H, H, 128)
     tile_cols = aligned(offset, TR, 128)
 
+    pairs = R // 2
+    twin = r + 1 - 2 * lax.rem(r, 2)
+    parity = lax.rem(r, 2)
+    group_index = r // 2
+
     def mate(d):
         return lax.rem(r + d, R)
+
+    def peer(e):
+        return lax.rem(r + 2 * e, R)
+
+    def sender_of(e):
+        return lax.rem(r + R - 2 * e, R)
 
     def remote(src, dst, send, recv, where):
         return pltpu.make_async_remote_copy(
@@ -107,53 +126,96 @@
 
         side.start()
 
+    def alt_copies(kind, i, wide):
+        wide_ref, near, _ = kinds[kind]
+        j = alternate.index((kind, i))
+        rows = aligned(i * chunk_rows, chunk_rows, chunk_rows)
+        kept = kept_rows.at[pl.ds(j * chunk_rows, chunk_rows)]
+        src = wide_ref.at[rows, alt_cols] if wide else kept
+        up = remote(src, kept, alt_up.at[j], alt_recv.at[j], (r, z + 1, p))
+        down = remote(src, kept, alt_down.at[j], alt_recv.at[j], (r, z - 1, p))
+        over = remote(kept, near.at[rows], alt_over.at[j], near_recv.at[kind, i], (alt, z, p))
+        return up, down, over
+
+    def pass_alt(kind, i, wide):
+        up, down, _ = alt_copies(kind, i, wide)
+
+        @pl.when(alt_has_up)
+        def _():
+            up.start()
+
+        @pl.when(alt_has_down)
+        def _():
+            down.start()
+
     def start_source(kind, i):
         @pl.when(is_source)
         def _():
-            pass_on(kind, i, True)
+            if (kind, i) in alternate:
+                near_copies(kind, i, True)[2].start()
+            else:
+                pass_on(kind, i, True)
+
+        if (kind, i) in alternate:
+            @pl.when(is_alt_source)
+            def _():
+                pass_alt(kind, i, True)
 
     def serve(kind, i):
+        if (kind, i) in alternate:
+            @pl.when(jnp.logical_not(is_alt_source))
+            def _():
+                alt_copies(kind, i, False)[0].wait_recv()
+                pass_alt(kind, i, False)
+                alt_copies(kind, i, False)[2].start()
+
         @pl.when(jnp.logical_not(is_source))
         def _():
             near_copies(kind, i, False)[0].wait_recv()
-            pass_on(kind, i, False)
+            if (kind, i) in alternate:
+                near_copies(kind, i, False)[2].start()
+            else:
+                pass_on(kind, i, False)
 
     def wait_far(kind, i):
         near_copies(kind, i, False)[2].wait_recv()
 
     def wait_sent(kind, i):
         up, down, side = near_copies(kind, i, False)
-
-        @pl.when(has_up)
+        side.wait_send()
+        if (kind, i) in alternate:
+            up, down, over = alt_copies(kind, i, False)
+
+            @pl.when(jnp.logical_not(is_alt_source))
+            def _():
+                over.wait_send()
+
+        rises, falls = (alt_has_up, alt_has_down) if (kind, i) in alternate else (has_up, has_down)
+
+        @pl.when(rises)
         def _():
             up.wait_send()
 
-        @pl.when(has_down)
+        @pl.when(falls)
         def _():
             down.wait_send()
-
-        side.wait_send()
 
     def xq_copy():
         rows = aligned(r * quarter, quarter, 8)
         return remote(samp.at[rows, far_cols], x_cols_far.at[rows], xq_send, xq_recv, across)
 
-    def xf_copy(d, sender):
-        rows = aligned(sender * quarter, quarter, 8)
-        return remote(x_cols_far.at[rows], x_cols_far.at[rows], xf_send.at[d], xf_recv.at[d], (mate(d), z, p))
-
-    def rs_copy(s, slot, d):
-        rows = aligned(mate(d) * piece, piece, 8)
+    def step_piece(s, owner):
+        return aligned(s * step_rows + owner * piece, piece, 8)
+
+    def pair_copy(s, slot, j):
+        rows = aligned((2 * j + 1 - parity) * piece, piece, 8)
         return remote(
-            partial.at[slot, rows], arrived.at[s, d - 1], rs_send.at[s, d], rs_recv.at[s, d], (mate(d), z, p)
+            partial.at[slot, rows], paired.at[s, j], pair_send.at[s, j], pair_recv.at[s, j], (twin, z, p)
         )
 
-    def step_piece(s, sender):
-        return aligned(s * step_rows + sender * piece, piece, 8)
-
-    def ag_copy(s, d, sender):
+    def rs_copy(s, e):
         return remote(
-            reduced.at[s], y_cols.at[step_piece(s, sender)], ag_send.at[s, d], ag_recv.at[s, d], (mate(d), z, p)
+            mid.at[s, peer(e) // 2], arrived.at[s, e - 1], rs_send.at[s, e], rs_recv.at[s, e], (peer(e), z, p)
         )
 
     def own_piece(s):
@@ -164,9 +226,48 @@
             reduced.at[s, :, far_cols], y_cols_far.at[step_piece(s, r)], yq_send.at[s], yq_recv.at[s], across
         )
 
-    def yf_copy(s, d, sender):
-        rows = step_piece(s, sender)
-        return remote(y_cols_far.at[rows], y_cols_far.at[rows], yf_send.at[s, d], yf_recv.at[s, d], (mate(d), z, p))
+    def shared(which, owner):
+        if which == 2 * steps:
+            return x_cols_far.at[aligned(owner * quarter, quarter, 8)]
+        if which < steps:
+            return y_cols.at[step_piece(which, owner)]
+        return y_cols_far.at[step_piece(which - steps, owner)]
+
+    def share_copy(which, e, owner, src=None):
+        piece_ref = shared(which, owner)
+        return remote(
+            piece_ref if src is None else src, piece_ref,
+            share_send.at[which, e], share_recv.at[which, e], (peer(e), z, p),
+        )
+
+    def hand_copy(which, owner, src=None):
+        piece_ref = shared(which, owner)
+        g = owner // 2
+        return remote(
+            piece_ref if src is None else src, piece_ref,
+            hand_send.at[which, g], hand_recv.at[which, g], (twin, z, p),
+        )
+
+    def share(which, src=None):
+        for e in range(1, pairs):
+            share_copy(which, e, r, src).start()
+        hand_copy(which, r, src).start()
+
+    def hand_on(which):
+        for e in range(1, pairs):
+            owner = sender_of(e)
+            share_copy(which, e, owner).wait_recv()
+            hand_copy(which, owner).start()
+
+    def wait_handed(which):
+        for g in range(pairs):
+            hand_copy(which, 2 * g + 1 - parity).wait_recv()
+
+    def wait_shared(which):
+        for e in range(1, pairs):
+            share_copy(which, e, r).wait_send()
+        for g in range(pairs):
+            hand_copy(which, 2 * g + parity).wait_send()
 
     for i in range(chunks):
         start_source(0, i)
@@ -177,40 +278,37 @@
         return pltpu.make_async_copy(prec.at[rows], left.at[slot, :, pl.ds(0, TC)], om_sem.at[slot])
 
     blocks = TR // depth
-    wide_block = block_of(TC)
-
-    def finish_rs(s, slot):
-        for d in range(1, R):
-            rs_copy(s, slot, d).wait_recv()
-        total = partial[slot, aligned(r * piece, piece, 8)]
-        for d in range(1, R):
-            total = total + arrived[s, d - 1]
+    wide_block = block_of(TC, 1024)
+
+    def combine(s, slot):
+        for j in range(pairs):
+            pair_copy(s, slot, j).wait_recv()
+            rows = aligned((2 * j + parity) * piece, piece, 8)
+            mid[s, j] = partial[slot, rows] + paired[s, j]
+        for e in range(1, pairs):
+            rs_copy(s, e).start()
+
+    def finish(s):
+        total = mid[s, group_index]
+        for e in range(1, pairs):
+            rs_copy(s, e).wait_recv()
+            total = total + arrived[s, e - 1]
         reduced[s] = total
         own_piece(s).start()
+        share(s, reduced.at[s])
         yq_copy(s).start()
-        for d in range(1, R):
-            ag_copy(s, d, r).start()
-
-    def wait_ag(s):
+
+    def source_step(s):
         own_piece(s).wait()
-        for d in range(1, R):
-            ag_copy(s, d, lax.rem(r + R - d, R)).wait_recv()
-
-    def source_step(s):
+        wait_handed(s)
         for j in range(per_step):
             start_source(1, s * per_step + j)
 
-    def forward_yf(s):
+    def spread_far(s):
         yq_copy(s).wait_recv()
-        for d in range(1, R):
-            yf_copy(s, d, r).start()
-
-    @pl.loop(0, steps)
-    def _(s):
-        slot = lax.rem(s, 2)
-        om_copy(0, 0).start()
-        for j in range(per_step):
-            serve(0, s * per_step + j)
+        share(steps + s)
+
+    def load_x(s):
         rows = aligned(s * step_rows, step_rows, step_rows)
 
         @pl.when(is_source)
@@ -221,13 +319,9 @@
         def _():
             pltpu.make_async_copy(x_near.at[rows], x_rows, load_sem.at[0]).start()
 
-        @pl.when(s >= 2)
-        def _():
-            for d in range(1, R):
-                rs_copy(s - 2, slot, d).wait_send()
-
         pltpu.make_async_copy(x_near.at[rows], x_rows, load_sem.at[0]).wait()
 
+    def products_step(slot):
         @pl.loop(0, blocks)
         def _(b):
             here = lax.rem(b, 2)
@@ -253,37 +347,61 @@
                 def _():
                     partial[slot, :, cols] += value
 
-        for d in range(1, R):
-            rs_copy(s, slot, d).start()
-
-        @pl.when(s >= 1)
-        def _():
-            finish_rs(s - 1, 1 - slot)
-
-        @pl.when(s == 1)
-        def _():
-            xq_copy().wait_recv()
-            for d in range(1, R):
-                xf_copy(d, r).start()
-
-        @pl.when(s >= 2)
-        def _():
-            wait_ag(s - 2)
-            source_step(s - 2)
-            forward_yf(s - 2)
-
-    last = steps - 1
-    serve(1, 0)
-    serve(1, 1)
-    finish_rs(last, last % 2)
-    wait_ag(last - 1)
-    source_step(last - 1)
-    forward_yf(last - 1)
-    serve(1, 2)
-    wait_ag(last)
-    source_step(last)
-    serve(1, 3)
-    forward_yf(last)
+    def products(s):
+        load_x(s)
+        if s >= 2:
+            for j in range(pairs):
+                pair_copy(s - 2, s % 2, j).wait_send()
+        products_step(s % 2)
+        for j in range(pairs):
+            pair_copy(s, s % 2, j).start()
+        if s + 1 < steps:
+            om_copy(0, 0).start()
+
+    def serve_x(i):
+        serve(0, i)
+
+    def serve_y(i):
+        serve(1, i)
+
+    def mix(s):
+        combine(s, s % 2)
+
+    def spread_x(_):
+        xq_copy().wait_recv()
+        share(2 * steps)
+
+    def hand_far(s):
+        hand_on(steps + s)
+
+    assert steps == 2 and chunks == 8
+    om_copy(0, 0).start()
+    order = (
+        (serve_x, 0), (serve_x, 1), (serve_x, 2), (serve_x, 7), (serve_x, 3), (products, 0), (serve_x, 5),
+        (mix, 0), (serve_x, 6), (finish, 0), (serve_x, 4), (hand_on, 0), (source_step, 0), (products, 1),
+        (mix, 1), (serve_y, 1), (serve_y, 0), (finish, 1),
+    )
+    for action, index in order:
+        action(index)
+    terms = (0, 1, 2, 4, 5, 3, 6, 7)
+    between = {
+        1: (
+            (spread_far, 0), (spread_x, 0), (hand_on, 1), (serve_y, 2), (serve_y, 3), (source_step, 1),
+            (spread_far, 1),
+        ),
+        2: (
+            (hand_far, 0), (hand_on, 2 * steps), (hand_far, 1), (serve_y, 4),
+        ),
+        3: (
+            (serve_y, 5),
+        ),
+        5: (
+            (serve_y, 6),
+        ),
+        6: (
+            (serve_y, 7),
+        ),
+    }
 
     m_block, n_block = block_of(TR), block_of(H)
     out_blocks = TR // m_block
@@ -310,17 +428,15 @@
 
         return run
 
-    def begin(u):
-        if u == 2:
-            for s in range(steps):
-                for d in range(1, R):
-                    yf_copy(s, d, lax.rem(r + R - d, R)).wait_recv()
-        if u == 5:
-            for d in range(1, R):
-                xf_copy(d, lax.rem(r + R - d, R)).wait_recv()
-        served = {1: (4,), 3: (5,), 5: (6, 7)}.get(u, ())
-        for i in served:
-            serve(1, i)
+    def begin(place):
+        u = terms[place]
+        for action, index in between.get(place, ()):
+            action(index)
+        if u in (2, 3):
+            for s in range(steps // 2):
+                wait_handed(steps + (u - 2) * (steps // 2) + s)
+        if u in (5, 7) and not {5, 7} & set(terms[:place]):
+            wait_handed(2 * steps)
         if u in (2, 3):
             for i in range(group):
                 wait_far(0, (u - 2) * group + i)
@@ -338,7 +454,7 @@
         else:
             load(y_far.at[rows], x_cols_far.at[rows])
 
-    assert halves == 2 and chunks == 8 and per_step == 2
+    assert halves == 2
 
     @pl.loop(0, 8)
     def _(u):
@@ -374,21 +490,20 @@
             def _():
                 out_copy(i).start()
 
-    @pl.loop(0, chunks)
-    def _(i):
+    for i in range(chunks):
         wait_sent(0, i)
         wait_sent(1, i)
 
     xq_copy().wait_send()
-    for d in range(1, R):
-        xf_copy(d, r).wait_send()
+    for which in range(2 * steps + 1):
+        wait_shared(which)
     for s in range(steps):
         yq_copy(s).wait_send()
-        for d in range(1, R):
-            if s >= steps - 2:
-                rs_copy(s, s % 2, d).wait_send()
-            ag_copy(s, d, r).wait_send()
-            yf_copy(s, d, r).wait_send()
+        for e in range(1, pairs):
+            rs_copy(s, e).wait_send()
+        if s >= steps - 2:
+            for j in range(pairs):
+                pair_copy(s, s % 2, j).wait_send()
 
     @pl.loop(0, out_blocks)
     def _(i):
@@ -402,9 +517,12 @@
     assert C > 2
     steps, chunks = S // step_rows, S // chunk_rows
     piece = step_rows // R
+    pairs, shares = R // 2, 2 * steps + 1
+    assert R % 2 == 0
     wide = max(TR, TC)
     dma = pltpu.SemaphoreType.DMA
     shapes = [(TR, H), (S, TR), (S, TR), (S, TR), (S, TR), (S, TC), (S, H), (S, H)]
+    shapes.append((len(alternate) * chunk_rows, TR))
     return pl.pallas_call(
         functools.partial(gather_kernel, R, C, S, TR, TC, H),
         out_shape=[jax.ShapeDtypeStruct(shape, F32) for shape in shapes],
@@ -418,11 +536,15 @@
             pltpu.VMEM((depth, H), BF16),
             pltpu.VMEM((step_rows, TR), F32),
             pltpu.VMEM((2, step_rows, TC), F32),
-            pltpu.VMEM((steps, R - 1, piece, TC), F32),
+            pltpu.VMEM((steps, pairs, piece, TC), F32),
+            pltpu.VMEM((steps, pairs, piece, TC), F32),
+            pltpu.VMEM((steps, pairs, piece, TC), F32),
             pltpu.VMEM((steps, piece, TC), F32),
             dma((2, chunks)), dma((2, chunks)), dma((2, chunks)), dma((2, chunks)), dma((2, chunks)),
-            dma((steps, R)), dma((steps, R)), dma((steps, R)), dma((steps, R)), dma((steps,)),
-            dma, dma, dma((R,)), dma((R,)), dma((steps,)), dma((steps,)), dma((steps, R)), dma((steps, R)),
+            dma((len(alternate),)), dma((len(alternate),)), dma((len(alternate),)), dma((len(alternate),)),
+            dma((steps, pairs)), dma((steps, pairs)), dma((steps, pairs)), dma((steps, pairs)), dma((steps,)),
+            dma((shares, pairs)), dma((shares, pairs)), dma((shares, pairs)), dma((shares, pairs)),
+            dma, dma, dma((steps,)), dma((steps,)),
             dma((2,)), dma((2,)), dma,
         ],
         compiler_params=pltpu.CompilerParams(

time: 493 us -> 444 us (0.901)
  Pallas kernels: 484 us -> 435 us
    pallas_call x1, Pallas kernels: 402 us -> 354 us  [gathered(): pl.pallas_call(functools.partial(gather_kernel, R, C, S, TR, TC, H), out_...]
where the time goes in v1:
time: 444 us; the launch traced here: 441 us
  Pallas kernels  435 us (98%)
  local copies, waits for them, and re-layouts  5.19 us (1%)
    pallas_call x1, Pallas kernels, gathered(): pl.pallas_call(functools.partial(gather_kernel, R, C, S, TR, TC, H), out_...  354 us
    pallas_call x1, Pallas kernels, residual_sum(): pl.pallas_call(functools.partial(residual_kernel, R), out_shape=jax.Shape...  45.7 us
    pallas_call x1, Pallas kernels, updated_and_partial(): pl.pallas_call(functools.partial(update_kernel, samples_total, block), ou...  35 us

profile of v1, /device:TPU:0, one launch (start us, length us, event | category | flops | bytes accessed | tf_op | source)
XLA Modules:
  0.0 441.5 jit_solution(9328084121869759727)
XLA Ops:
  0.6 0.6 pad_add_fusion.ids
  1.2 0.0 copy-start.1
  1.3 354.3 %gather_symmetric.1 = (f32[3072,1536]{1,0:T(8,128)}, f32[512,3072]{1,0:T(8,128)}, f32[512,3072]{1,0:T(8,128)}, f32[512,3072]{1,0:T(8,128)}, f32[512,3072]{1,0:T(...) custom-call(f32[3072,3072]{1,0:T(8,128)} %prec.3, f32[512,3072]{1,0:T(8,128)} %samp.1), custom_call_target="tpu_custom_call" | custom-call | tf_op jit(solution)/shard_map/gather_symmetric/pallas_call | solution.py:526
  355.5 0.0 copy-done.1
  355.6 1.7 copy.6.rows_o
  357.3 0.1 dynamic_slice.7
  357.4 0.6 broadcast_in_dim.7.cols_o
  357.9 35.0 %update_rows.1 = (f32[3072,1536]{1,0:T(8,128)}, f32[520,1536]{1,0:T(8,128)}) custom-call(s32[3]{0:T(128)} %pad_add_fusion.ids, f32[3072,1536]{1,0:T(8,128)} %get-tuple-element.5.sym, f32[3072,3072]{1,0:T(8,128)} %prec.3, f32[3072,1]{1,0:T(8,128)} %copy.6.rows_o, f32[1,1536]{1,0:T(1,128)} %broadcast_in_dim.7.cols_o, f32[512,3072]{1,0:T(8,128)} %new_t.1), custom_call_target="tpu_custom_call" | custom-call | tf_op jit(solution)/shard_map/update_rows/pallas_call | solution.py:595
  393.0 0.0 copy-start
  393.0 1.9 copy-done
  394.9 45.7 %residual_sum.1 = f32[128,1536]{1,0:T(8,128)S(1)} custom-call(f32[520,1536]{1,0:T(8,128)S(1)} %copy-done), custom_call_target="tpu_custom_call" | custom-call | tf_op jit(solution)/shard_map/residual_sum/pallas_call | solution.py:688
  440.6 0.9 copy.8
  (2 shorter events, 0.0 us)
Async XLA Ops:
  1.2 354.3 %copy-start.1 = (s32[12288]{0:T(1024)S(1)}, s32[12288]{0:T(1024)}, u32[]{:S(2)}) copy-start(s32[12288]{0:T(1024)} %param.7) | copy-start | bytes 147460
  393.0 1.9 copy-start

commit v2 on v1

--- a/solution.py
+++ b/solution.py
@@ -15,7 +15,7 @@
 step_rows = 256
 chunk_rows = 64
 depth = 256
-alternate = ((0, 5), (0, 7))
+alternate = ((0, 3), (0, 7))
 
 
 def block_of(size, most=512):
@@ -377,26 +377,22 @@
     assert steps == 2 and chunks == 8
     om_copy(0, 0).start()
     order = (
-        (serve_x, 0), (serve_x, 1), (serve_x, 2), (serve_x, 7), (serve_x, 3), (products, 0), (serve_x, 5),
-        (mix, 0), (serve_x, 6), (finish, 0), (serve_x, 4), (hand_on, 0), (source_step, 0), (products, 1),
-        (mix, 1), (serve_y, 1), (serve_y, 0), (finish, 1),
+        (serve_x, 0), (serve_x, 1), (serve_x, 2), (serve_x, 3), (products, 0), (serve_x, 6), (serve_x, 7),
+        (mix, 0), (finish, 0), (serve_x, 5), (hand_on, 0), (serve_x, 4), (source_step, 0), (products, 1),
+        (mix, 1), (serve_y, 1), (serve_y, 0), (finish, 1), (spread_x, 0),
     )
     for action, index in order:
         action(index)
-    terms = (0, 1, 2, 4, 5, 3, 6, 7)
+    terms = (0, 1, 4, 2, 5, 3, 6, 7)
     between = {
         1: (
-            (spread_far, 0), (spread_x, 0), (hand_on, 1), (serve_y, 2), (serve_y, 3), (source_step, 1),
-            (spread_far, 1),
-        ),
-        2: (
-            (hand_far, 0), (hand_on, 2 * steps), (hand_far, 1), (serve_y, 4),
+            (hand_on, 1), (serve_y, 2), (serve_y, 3), (spread_far, 0), (source_step, 1), (spread_far, 1),
         ),
         3: (
-            (serve_y, 5),
+            (hand_far, 0), (hand_far, 1), (hand_on, 2 * steps), (serve_y, 5), (serve_y, 6),
         ),
         5: (
-            (serve_y, 6),
+            (serve_y, 4),
         ),
         6: (
             (serve_y, 7),
@@ -557,41 +553,43 @@
 def update_kernel(samples_total, block, ids, sym, prec, rows_o, cols_o, new_t, out, res):
     i = pl.program_id(0)
     M, H = sym.shape
-    row_id = ids[0] + i * block + lax.broadcasted_iota(jnp.int32, (M, H), 0)
-    col_id = ids[1] + lax.broadcasted_iota(jnp.int32, (M, H), 1)
-    on_diagonal = row_id == col_id
-    held = prec[...]
-    inverse = jnp.where(on_diagonal, 1.0 / jnp.where(on_diagonal, held, 1.0), 0.0)
-    gradient = sym[...] / (2.0 * samples_total) - inverse
-    stepped = held - step_size * gradient
-    threshold = step_size * penalty * 0.5 * (rows_o[...] + cols_o[...])
-    size = jnp.maximum(jnp.abs(stepped) - threshold, 0.0)
-    shrunk = jnp.where(stepped < 0.0, -size, size)
-    updated = jnp.where(on_diagonal, stepped, shrunk)
-    out[...] = updated
-    u_high, u_low = split(updated)
-    n_high, n_low = split(new_t[...])
-    count = n_high.shape[0]
-    pair = dot(jnp.concatenate([n_high, n_low], axis=0), u_high)
-    value = pair[:count] + pair[count:] + dot(n_high, u_low)
-    diag = jnp.sum(jnp.where(on_diagonal, held, 0.0), axis=0, keepdims=True)
-    diag = jnp.broadcast_to(diag, (8, H))
+    count = new_t.shape[0]
 
     @pl.when(i == 0)
     def _():
-        res[pl.ds(0, count), :] = value
-        res[pl.ds(count, 8), :] = diag
-
-    @pl.when(i > 0)
-    def _():
-        res[pl.ds(0, count), :] += value
-        res[pl.ds(count, 8), :] += diag
+        res[...] = jnp.zeros_like(res)
+
+    n_high, n_low = split(new_t[...])
+    both = jnp.concatenate([n_high, n_low], axis=0)
+    wide = block_of(H)
+    row_id = ids[0] + i * block + lax.broadcasted_iota(jnp.int32, (M, wide), 0)
+    order_rows = rows_o[...].T[:, :1]
+    for n in range(H // wide):
+        cols = pl.ds(n * wide, wide)
+        col_id = ids[1] + n * wide + lax.broadcasted_iota(jnp.int32, (M, wide), 1)
+        on_diagonal = row_id == col_id
+        held = prec[:, cols]
+        diag = jnp.sum(jnp.where(on_diagonal, held, 0.0), axis=0, keepdims=True)
+        inverse = jnp.where(on_diagonal, 1.0 / diag, 0.0)
+        gradient = sym[:, cols] / (2.0 * samples_total) - inverse
+        stepped = held - step_size * gradient
+        threshold = step_size * penalty * 0.5 * (order_rows + cols_o[:, cols])
+        size = jnp.maximum(jnp.abs(stepped) - threshold, 0.0)
+        shrunk = jnp.where(stepped < 0.0, -size, size)
+        updated = jnp.where(on_diagonal, stepped, shrunk)
+        out[:, cols] = updated
+        u_high, u_low = split(updated)
+        pair = dot(both, u_high)
+        value = pair[:count] + pair[count:] + dot(n_high, u_low)
+        res[pl.ds(0, count), cols] += value
+        res[pl.ds(count, 8), cols] += jnp.broadcast_to(diag, (8, wide))
 
 
 def updated_and_partial(symmetric, precision, new_rows, orders_rows, orders_cols, ids, half_index, samples_total):
     TR, H = symmetric.shape
     count = new_rows.shape[0]
     block = 256
+
     return pl.pallas_call(
         functools.partial(update_kernel, samples_total, block),
         out_shape=[jax.ShapeDtypeStruct((TR, H), F32), jax.ShapeDtypeStruct((count + 8, H), F32)],
@@ -601,7 +599,7 @@
             in_specs=[
                 pl.BlockSpec((block, H), lambda i, ids: (i, 0)),
                 pl.BlockSpec((block, H), lambda i, ids: (i, ids[2])),
-                pl.BlockSpec((block, 1), lambda i, ids: (i, 0)),
+                pl.BlockSpec((8, block), lambda i, ids: (0, i)),
                 pl.BlockSpec((1, H), lambda i, ids: (0, 0)),
                 pl.BlockSpec((count, block), lambda i, ids: (0, i)),
             ],
@@ -712,7 +710,7 @@
     symmetric = gathered(precision, samples, R, C)
     orders = ngram_order.astype(F32)
     row_start, col_start = r * TR, c * TC + p * H
-    order_rows = lax.dynamic_slice_in_dim(orders, row_start, TR, 0)[:, None]
+    order_rows = jnp.broadcast_to(lax.dynamic_slice_in_dim(orders, row_start, TR, 0)[None, :], (8, TR))
     order_cols = lax.dynamic_slice_in_dim(orders, col_start, H, 0)[None, :]
     ids = jnp.stack([row_start, col_start, p]).astype(jnp.int32)
     updated, part = updated_and_partial(

time: 444 us -> 430 us (0.968)
  Pallas kernels: 435 us -> 425 us
    pallas_call x1, Pallas kernels: 354 us -> 344 us  [gathered(): pl.pallas_call(functools.partial(gather_kernel, R, C, S, TR, TC, H), out_...]
    pallas_call x1, Pallas kernels: 35 us -> 29 us  [updated_and_partial(): pl.pallas_call(functools.partial(update_kernel, samples_total, block), ou...]
    pallas_call x1, Pallas kernels: 45.7 us -> 51.2 us  [residual_sum(): pl.pallas_call(functools.partial(residual_kernel, R), out_shape=jax.Shape...]
where the time goes in v2:
time: 430 us
  Pallas kernels  425 us (99%)
    pallas_call x1, Pallas kernels, gathered(): pl.pallas_call(functools.partial(gather_kernel, R, C, S, TR, TC, H), out_...  344 us
    pallas_call x1, Pallas kernels, residual_sum(): pl.pallas_call(functools.partial(residual_kernel, R), out_shape=jax.Shape...  51.2 us
    pallas_call x1, Pallas kernels, updated_and_partial(): pl.pallas_call(functools.partial(update_kernel, samples_total, block), ou...  29 us

profile of v2, /device:TPU:0, one launch (start us, length us, event | category | flops | bytes accessed | tf_op | source)
XLA Modules:
  0.0 430.0 jit_solution(10104071183490913473)
XLA Ops:
  0.6 0.6 pad_add_fusion.ids
  1.2 0.0 copy-start.1
  1.3 344.4 %gather_symmetric.1 = (f32[3072,1536]{1,0:T(8,128)}, f32[512,3072]{1,0:T(8,128)}, f32[512,3072]{1,0:T(8,128)}, f32[512,3072]{1,0:T(8,128)}, f32[512,3072]{1,0:T(...) custom-call(f32[3072,3072]{1,0:T(8,128)} %prec.3, f32[512,3072]{1,0:T(8,128)} %samp.1), custom_call_target="tpu_custom_call" | custom-call | tf_op jit(solution)/shard_map/gather_symmetric/pallas_call | solution.py:522
  345.6 0.0 copy-done.1
  345.7 0.6 broadcast_in_dim.4.rows_o
  346.3 0.1 dynamic_slice.7
  346.4 0.6 broadcast_in_dim.10.cols_o
  347.0 29.0 %update_rows.1 = (f32[3072,1536]{1,0:T(8,128)}, f32[520,1536]{1,0:T(8,128)}) custom-call(s32[3]{0:T(128)} %pad_add_fusion.ids, f32[3072,1536]{1,0:T(8,128)} %get-tuple-element.5.sym, f32[3072,3072]{1,0:T(8,128)} %prec.3, f32[8,3072]{1,0:T(8,128)} %broadcast_in_dim.4.rows_o, f32[1,1536]{1,0:T(1,128)} %broadcast_in_dim.10.cols_o, f32[512,3072]{1,0:T(8,128)} %new_t.1), custom_call_target="tpu_custom_call" | custom-call | tf_op jit(solution)/shard_map/update_rows/pallas_call | solution.py:593
  376.0 0.0 copy-start
  376.1 1.9 copy-done
  378.0 51.2 %residual_sum.1 = f32[128,1536]{1,0:T(8,128)S(1)} custom-call(f32[520,1536]{1,0:T(8,128)S(1)} %copy-done), custom_call_target="tpu_custom_call" | custom-call | tf_op jit(solution)/shard_map/residual_sum/pallas_call | solution.py:686
  429.1 0.9 copy.7
  (2 shorter events, 0.0 us)
Async XLA Ops:
  1.2 344.4 %copy-start.1 = (s32[12288]{0:T(1024)S(1)}, s32[12288]{0:T(1024)}, u32[]{:S(2)}) copy-start(s32[12288]{0:T(1024)} %param.7) | copy-start | bytes 147460
  376.0 1.9 copy-start

commit v3 on v2

--- a/solution.py
+++ b/solution.py
@@ -645,13 +645,19 @@
             device_id=(peer, z, p), device_id_type=MESH)
 
     count = [R >> (stage + 1) for stage in range(rounds)]
+    def ranked(stage):
+        if stage + 1 == rounds:
+            return [0], []
+        own = lax.rem(r // (2 << stage), 2)
+        first = [2 * j + 1 - own for j in range(count[stage + 1])]
+        return first, [2 * j + own for j in range(count[stage + 1])]
+
+    for j in sum(ranked(0), []):
+        exchange(0, j).start()
+    for d in range(1, R):
+        diag_copy(d).start()
     for stage in range(rounds):
         bit = 1 << stage
-        if stage == 0:
-            for j in range(count[0]):
-                exchange(0, j).start()
-            for d in range(1, R):
-                diag_copy(d).start()
 
         def receive(j, stage=stage, bit=bit):
             mine = lax.rem(r, 2 * bit) + 2 * bit * j
@@ -660,11 +666,13 @@
             src = part if stage == 0 else held
             held[block] = src[block] + got[stage, j]
 
-        for j in range(count[stage]):
-            receive(j)
-        if stage + 1 < rounds:
-            for j in range(count[stage + 1]):
+        first, second = ranked(stage)
+        for j, index in enumerate(first):
+            receive(index)
+            if stage + 1 < rounds:
                 exchange(stage + 1, j).start()
+        for index in second:
+            receive(index)
     diag = part[pl.ds(rows * R, 1)]
     for d in range(1, R):
         diag_copy(d).wait_recv()

time: 430 us -> 429 us (level)
  no operation moved by 1% of the time
where the time goes in v3:
time: 429 us
  Pallas kernels  423 us (99%)
    pallas_call x1, Pallas kernels, gathered(): pl.pallas_call(functools.partial(gather_kernel, R, C, S, TR, TC, H), out_...  344 us
    pallas_call x1, Pallas kernels, residual_sum(): pl.pallas_call(functools.partial(residual_kernel, R), out_shape=jax.Shape...  50 us
    pallas_call x1, Pallas kernels, updated_and_partial(): pl.pallas_call(functools.partial(update_kernel, samples_total, block), ou...  29 us

profile of v3, /device:TPU:0, one launch (start us, length us, event | category | flops | bytes accessed | tf_op | source)
XLA Modules:
  0.0 428.9 jit_solution(7212921757476252026)
XLA Ops:
  0.6 0.6 pad_add_fusion.ids
  1.2 0.0 copy-start.1
  1.3 344.4 %gather_symmetric.1 = (f32[3072,1536]{1,0:T(8,128)}, f32[512,3072]{1,0:T(8,128)}, f32[512,3072]{1,0:T(8,128)}, f32[512,3072]{1,0:T(8,128)}, f32[512,3072]{1,0:T(...) custom-call(f32[3072,3072]{1,0:T(8,128)} %prec.3, f32[512,3072]{1,0:T(8,128)} %samp.1), custom_call_target="tpu_custom_call" | custom-call | tf_op jit(solution)/shard_map/gather_symmetric/pallas_call | solution.py:522
  345.6 0.0 copy-done.1
  345.7 0.6 broadcast_in_dim.4.rows_o
  346.3 0.1 dynamic_slice.7
  346.4 0.6 broadcast_in_dim.10.cols_o
  347.0 29.0 %update_rows.1 = (f32[3072,1536]{1,0:T(8,128)}, f32[520,1536]{1,0:T(8,128)}) custom-call(s32[3]{0:T(128)} %pad_add_fusion.ids, f32[3072,1536]{1,0:T(8,128)} %get-tuple-element.5.sym, f32[3072,3072]{1,0:T(8,128)} %prec.3, f32[8,3072]{1,0:T(8,128)} %broadcast_in_dim.4.rows_o, f32[1,1536]{1,0:T(1,128)} %broadcast_in_dim.10.cols_o, f32[512,3072]{1,0:T(8,128)} %new_t.1), custom_call_target="tpu_custom_call" | custom-call | tf_op jit(solution)/shard_map/update_rows/pallas_call | solution.py:593
  376.0 0.0 copy-start
  376.1 1.9 copy-done
  378.0 50.0 %residual_sum.1 = f32[128,1536]{1,0:T(8,128)S(1)} custom-call(f32[520,1536]{1,0:T(8,128)S(1)} %copy-done), custom_call_target="tpu_custom_call" | custom-call | tf_op jit(solution)/shard_map/residual_sum/pallas_call | solution.py:694
  428.0 0.9 copy.7
  (2 shorter events, 0.0 us)
Async XLA Ops:
  1.2 344.4 %copy-start.1 = (s32[12288]{0:T(1024)S(1)}, s32[12288]{0:T(1024)}, u32[]{:S(2)}) copy-start(s32[12288]{0:T(1024)} %param.7) | copy-start | bytes 147460
  376.0 1.9 copy-start
